TPU v7x, 32 devices: a whole 2x2x4 slice. The times are simulated.
32 devices in a mesh: tm: 4 (over y, x), pts: 8 (over z, core).
Axes of the slice: x: 2, y: 2, z: 4, core: 2. Of those that a mesh axis runs over, the one named last changes fastest.
Arguments:
- orbitals: bfloat16 [8192, 2048], P('pts'), may hold values from -6 to 6
- panel_orbitals: bfloat16 [1024, 2048], P(('tm', 'pts')), may hold values from -0.1796875 to 0.1796875
- band_gap: float32 [2048], replicated, may hold values from 0.1 to 1
- tau_points: float32 [4], replicated, may hold values from 0.1 to 2
- quad_weight: float32 [4], replicated, may hold values from 0.1 to 1
- frequencies: float32 [8], replicated, may hold values from 0.1 to 3
- coulomb: bfloat16 [1024, 1024], P(('tm', 'pts')), may hold values from -0.1875 to 0.1875
Outputs:
- screened: bfloat16 [8, 8192, 1024], P(None, ('pts', 'tm'))
All inputs are finite; a program needn't handle non-finite values.
Results may differ from a plain program's by a relative error of at most 0.0056.
Values may be sent and summed in bfloat16 or wider, within the bound.
A program may use at most 64 MiB of HBM per device.

v0:
```python
import jax
import jax.numpy as jnp
from jax import lax
from jax.sharding import PartitionSpec as P

NOCC = 512
PANEL = 1024
TAU_DEV = 1
FREQS = 8


def contract(left, right):
    return lax.dot_general(
        left, right, (((1,), (1,)), ((), ())), preferred_element_type=jnp.float32
    )


def shards(orbitals, panel_orbitals, band_gap, tau_points, quad_weight, frequencies, coulomb):
    group = lax.axis_index("tm")
    own_taus = lax.dynamic_slice_in_dim(tau_points, group * TAU_DEV, TAU_DEV)
    decay = jnp.exp(-band_gap[None, :] * own_taus[:, None])
    occ_rows = orbitals[:, :NOCC]
    vir_rows = orbitals[:, NOCC:]
    widened = lax.all_gather(panel_orbitals, ("tm", "pts"), axis=0, tiled=True).astype(jnp.float32)
    scaled = (widened * decay[0][None, :]).astype(jnp.bfloat16)
    green_occ = contract(occ_rows, scaled[:, :NOCC])
    green_vir = contract(vir_rows, scaled[:, NOCC:])
    layers = [(-(green_occ * green_vir)).astype(jnp.bfloat16)]
    polar = jnp.stack(layers)
    regrouped = lax.all_to_all(polar, "tm", split_axis=1, concat_axis=0, tiled=True)
    times_all = regrouped.shape[0]
    row_count = regrouped.shape[1]
    cosines = quad_weight[None, :] * jnp.cos(frequencies[:, None] * tau_points[None, :])
    flat = regrouped.reshape(times_all, row_count * PANEL).astype(jnp.float32)
    transformed = jnp.dot(cosines, flat, precision=lax.Precision.HIGHEST).astype(jnp.bfloat16)
    transformed = transformed.reshape(FREQS * row_count, PANEL)
    whole_block = lax.all_gather(coulomb, ("tm", "pts"), axis=0, tiled=True)
    screened = jnp.dot(transformed, whole_block, preferred_element_type=jnp.float32)
    return screened.astype(jnp.bfloat16).reshape(FREQS, row_count, PANEL)


def solution(mesh):
    placed = (P("pts", None), P(("tm", "pts"), None), P(), P(), P(), P(), P(("tm", "pts"), None))
    return jax.shard_map(
        shards, mesh=mesh, in_specs=placed, out_specs=P(None, ("pts", "tm"), None), check_vma=False
    )
```

profile of v0, /device:TPU:0, one launch (start us, length us, event | category | flops | bytes accessed | tf_op | source)
XLA Modules:
  0.0 188.5 jit_solution(1147528016978019313)
XLA Ops:
  6.5 0.0 all-gather.3.cloned.1.call-start
  6.5 0.7 all-gather.3.cloned.1.call-update
  7.3 0.0 all-gather.5.cloned.1.call-start
  7.3 0.7 all-gather.5.cloned.1.call-update
  8.0 1.2 dynamic_slice.3
  9.3 1.3 multiply_exponential_fusion
  10.6 64.2 %all-gather.3.cloned.1.call-done = bf16[1024,2048]{1,0:T(8,128)(2,1)} async-done(((bf16[32,2048]{1,0:T(8,128)(2,1)}), bf16[1024,2048]{1,0:T(8,128)(2,1)}) %all-gather.3.cloned.1.call-update) | async-done | bytes 4194320 | tf_op jit(solution)/shard_map/all_gather | solution.py:24
  74.8 0.0 copy-start
  74.8 3.4 %multiply_convert_fusion = bf16[1024,2048]{1,0:T(8,128)(2,1)S(1)} fusion(bf16[1024,2048]{1,0:T(8,128)(2,1)} %all-gather.3.cloned.1.call-done, f32[2048]{0:T(1024)S(1)} %multiply_exponential_fusion), kind=kLoop, calls=%fused_computation.1 | loop fusion | flops 6291456 | bytes 8396800 | tf_op jit(solution)/shard_map/convert_element_type | solution.py:25
  78.2 0.0 copy-done
  78.2 3.5 %fusion = f32[1024,1024]{1,0:T(8,128)S(1)} fusion(bf16[1024,2048]{1,0:T(8,128)(2,1)S(1)} %multiply_convert_fusion, bf16[1024,2048]{1,0:T(8,128)(2,1)S(1)} %copy-done), kind=kOutput, calls=%fused_computation.4 | convolution fusion | flops 3221225472 | bytes 10485760 | tf_op jit(solution)/shard_map/dot_general | solution.py:13
  81.7 1.3 fusion.3
  83.0 7.5 %copy.9 = bf16[1,1024,1024]{2,0,1:T(2,128)(2,1)} copy(bf16[1,1024,1024]{1,2,0:T(8,128)(2,1)S(1)} %fusion.3) | data formatting | bytes 4194304 | tf_op jit(solution)/shard_map/stack | solution.py:29
  90.5 0.5 broadcast.7
  91.1 12.8 %reduce.2 = bf16[1024,1024]{1,0:T(8,128)(2,1)S(1)} reduce(bf16[1024,1,1024]{2,1,0:T(2,128)(2,1)} %bitcast.12, bf16[]{:T(256)} %broadcast.7), dimensions={1}, to_apply=%bitcast.6.reduce_sub_computation | reduce | bytes 4194306
  103.8 2.8 %reshape.27 = bf16[4,2,131072]{2,1,0:T(2,128)(2,1)} reshape(bf16[1024,1024]{1,0:T(8,128)(2,1)S(1)} %reduce.2) | data formatting | bytes 4194304
  106.6 33.3 %all_to_all.4 = bf16[4,2,131072]{2,1,0:T(2,128)(2,1)S(1)} all-to-all(bf16[4,2,131072]{2,1,0:T(2,128)(2,1)} %reshape.27), channel_id=1, replica_groups=mesh['tm'=4,'pts'=8] {'tm'}, dimensions={0} | all-to-all | bytes 4194304 | tf_op jit(solution)/shard_map/all_to_all | solution.py:30
  139.9 3.3 %reshape.28 = bf16[1024,1,1024]{2,1,0:T(2,128)(2,1)} reshape(bf16[4,2,131072]{2,1,0:T(2,128)(2,1)S(1)} %all_to_all.4) | data formatting | bytes 4194304
  143.2 0.0 copy-start.1
  143.2 0.0 copy-start.2
  143.2 0.0 copy-start.3
  143.2 14.7 %bitcast_reduce_fusion = bf16[1024,1024]{1,0:T(8,128)(2,1)} fusion(bf16[1024,1,1024]{2,1,0:T(2,128)(2,1)} %reshape.28), kind=kLoop, calls=%fused_computation.17 | loop fusion | bytes 4194304 | tf_op jit(solution)/shard_map/all_to_all | solution.py:30
  157.9 3.2 %reshape.23 = bf16[4,262144]{1,0:T(4,128)(2,1)S(1)} reshape(bf16[1024,1024]{1,0:T(8,128)(2,1)} %bitcast_reduce_fusion) | data formatting | bytes 4194304 | tf_op jit(solution)/shard_map/reshape | solution.py:34
  161.1 0.0 copy-done.1
  161.1 0.0 copy-done.2
  161.1 0.0 copy-done.3
  161.1 5.1 %convolution_convert_fusion = bf16[8,262144]{1,0:T(8,128)(2,1)} fusion(bf16[4,262144]{1,0:T(4,128)(2,1)S(1)} %reshape.23, f32[4]{0:T(128)S(1)} %copy-done.1, f32[8]{0:T(128)S(1)} %copy-done.2, f32[4]{0:T(128)S(1)} %copy-done.3), kind=kOutput, calls=%fused_computation | convolution fusion | flops 102760512 | bytes 6291520 | tf_op jit(solution)/shard_map/dot_general | solution.py:35
  166.2 6.0 %reshape.24 = bf16[2048,1024]{1,0:T(8,128)(2,1)} reshape(bf16[8,262144]{1,0:T(8,128)(2,1)} %convolution_convert_fusion) | data formatting | bytes 8388608 | tf_op jit(solution)/shard_map/reshape | solution.py:36
  172.2 0.0 all-gather.5.cloned.1.call-done
  172.2 9.4 %convolution_convert_fusion.1 = bf16[2048,1024]{1,0:T(8,128)(2,1)} fusion(bf16[2048,1024]{1,0:T(8,128)(2,1)} %reshape.24, bf16[1024,1024]{1,0:T(8,128)(2,1)} %all-gather.5.cloned.1.call-done), kind=kOutput, calls=%fused_computation.3 | convolution fusion | flops 4297064448 | bytes 10485760 | tf_op jit(solution)/shard_map/dot_general | solution.py:38
Async XLA Ops:
  6.5 68.2 %all-gather.3.cloned.1.call-start = ((), (), s32[]{:S(2)}) async-start(), calls=%async_computation.1 | async-start | bytes 4325376 | tf_op jit(solution)/shard_map/all_gather | solution.py:24
  7.3 165.0 %all-gather.5.cloned.1.call-start = ((), (), s32[]{:S(2)}) async-start(), calls=%async_computation.2 | async-start | bytes 2162688 | tf_op jit(solution)/shard_map/all_gather | solution.py:37
  74.8 3.5 %copy-start = (bf16[1024,2048]{1,0:T(8,128)(2,1)S(1)}, bf16[1024,2048]{1,0:T(8,128)(2,1)}, u32[]{:S(2)}) copy-start(bf16[1024,2048]{1,0:T(8,128)(2,1)} %param.7) | copy-start | bytes 12582916
  143.2 17.9 %copy-start.1 = (f32[4]{0:T(128)S(1)}, f32[4]{0:T(128)}, u32[]{:S(2)}) copy-start(f32[4]{0:T(128)} %param.10) | copy-start | bytes 52
  143.2 17.9 %copy-start.2 = (f32[8]{0:T(128)S(1)}, f32[8]{0:T(128)}, u32[]{:S(2)}) copy-start(f32[8]{0:T(128)} %param.12) | copy-start | bytes 100
  143.2 17.9 %copy-start.3 = (f32[4]{0:T(128)S(1)}, f32[4]{0:T(128)}, u32[]{:S(2)}) copy-start(f32[4]{0:T(128)} %param.11) | copy-start | bytes 52
Sparse Core Ops, SparseCore 0:
  10.3 64.3 all-gather.2
  77.7 60.9 all-gather.4
where the time goes:
time: 189 us; the launch traced here: 188 us
  waiting for transfers between devices  65.6 us (35%)
  local copies, waits for them, and re-layouts  39.2 us (21%)
  blocking collectives  33.3 us (18%)
  matrix products  19.3 us (10%)
  other arithmetic  17.5 us (9%)
  between operations  13.5 us (7%)
    all_gather x1, waiting for transfers between devices, shards(): lax.all_gather(panel_orbitals, ('tm', 'pts'), axis=0, tiled=True)  64.2 us
    all_to_all x1, blocking collectives, shards(): lax.all_to_all(polar, 'tm', split_axis=1, concat_axis=0, tiled=True)  33.3 us
    all_to_all x1, local copies, waits for them, and re-layouts, shards(): lax.all_to_all(polar, 'tm', split_axis=1, concat_axis=0, tiled=True)  14.7 us
    unnamed x1, other arithmetic  12.8 us
    dot_general x1, matrix products, shards(): jnp.dot(transformed, whole_block, preferred_element_type=jnp.float32)  9.41 us
    another operation x1, local copies, waits for them, and re-layouts, shards(): polar = jnp.stack(layers)  7.52 us
    unnamed x11, local copies, waits for them, and re-layouts  6.57 us
    reshape x1, local copies, waits for them, and re-layouts, shards(): transformed = transformed.reshape(FREQS * row_count, PANEL)  6.02 us
  transfers between devices with their start and end apart: 2, of which 1 were waited for; matrix products, arithmetic and copies ran while one was open for 35% of the time, Pallas kernels for 0%

commit v1 on v0

--- a/solution.py
+++ b/solution.py
@@ -27,7 +27,15 @@
     green_vir = contract(vir_rows, scaled[:, NOCC:])
     layers = [(-(green_occ * green_vir)).astype(jnp.bfloat16)]
     polar = jnp.stack(layers)
-    regrouped = lax.all_to_all(polar, "tm", split_axis=1, concat_axis=0, tiled=True)
+    regrouped = jnp.concatenate(
+        lax.all_to_all(
+            jnp.stack(jnp.split(polar, lax.axis_size("tm"), axis=1)),
+            axis_name="tm",
+            split_axis=0,
+            concat_axis=0,
+        ),
+        axis=0,
+    )
     times_all = regrouped.shape[0]
     row_count = regrouped.shape[1]
     cosines = quad_weight[None, :] * jnp.cos(frequencies[:, None] * tau_points[None, :])

time: 189 us -> 151 us (0.80)
  local copies, waits for them, and re-layouts: 39.2 us -> 13 us
  other arithmetic: 17.5 us -> 5.05 us
  waiting for transfers between devices: 65.6 us -> 69.6 us
  blocking collectives: 33.3 us -> 30.4 us
    unnamed x1 -> x0, other arithmetic: 12.8 us -> none
    all_to_all x1, local copies, waits for them, and re-layouts: 14.7 us -> 2.37 us  [shards(): lax.all_to_all(jnp.stack(jnp.split(polar, lax.axis_size('tm'), axis=1)),...]
    another operation x1, local copies, waits for them, and re-layouts: 7.52 us -> 0.14 us  [shards(): jnp.stack(jnp.split(polar, lax.axis_size('tm'), axis=1))]
    all_gather x1, waiting for transfers between devices: 0.01 us -> 4.07 us  [shards(): whole_block = lax.all_gather(coulomb, ('tm', 'pts'), axis=0, tiled=True)]
    unnamed x11 -> x9, local copies, waits for them, and re-layouts: 6.57 us -> 3.23 us
    reshape x1 -> x0, local copies, waits for them, and re-layouts: 3.2 us -> none  [shards(): flat = regrouped.reshape(times_all, row_count * PANEL).astype(jnp.float32)]
    all_to_all x1, blocking collectives: 33.3 us -> 30.4 us  [shards(): lax.all_to_all(jnp.stack(jnp.split(polar, lax.axis_size('tm'), axis=1)),...]
  transfers between devices with their start and end apart: 2 -> 2, of which waited for: 1 -> 2; matrix products, arithmetic and copies ran while one was open for 35% -> 19% of each run, Pallas kernels for 0% -> 0%
where the time goes in v1:
time: 151 us
  waiting for transfers between devices  69.6 us (46%)
  blocking collectives  30.4 us (20%)
  matrix products  19.3 us (13%)
  between operations  13.5 us (9%)
  local copies, waits for them, and re-layouts  13 us (9%)
  other arithmetic  5.05 us (3%)
    all_gather x1, waiting for transfers between devices, shards(): lax.all_gather(panel_orbitals, ('tm', 'pts'), axis=0, tiled=True)  64.2 us
    all_to_all x1, blocking collectives, shards(): lax.all_to_all(jnp.stack(jnp.split(polar, lax.axis_size('tm'), axis=1)),...  30.4 us
    dot_general x1, matrix products, shards(): jnp.dot(transformed, whole_block, preferred_element_type=jnp.float32)  9.41 us
    reshape x1, local copies, waits for them, and re-layouts, shards(): transformed = transformed.reshape(FREQS * row_count, PANEL)  6.04 us
    dot_general x1, matrix products, shards(): jnp.dot(cosines, flat, precision=lax.Precision.HIGHEST).astype(jnp.bfloat16)  5.12 us
    dot_general x2, matrix products, contract(): lax.dot_general(left, right, (((1,), (1,)), ((), ())), preferred_element_...  4.78 us
    all_gather x1, waiting for transfers between devices, shards(): whole_block = lax.all_gather(coulomb, ('tm', 'pts'), axis=0, tiled=True)  4.07 us
    convert_element_type x1, other arithmetic, shards(): scaled = (widened * decay[0][None, :]).astype(jnp.bfloat16)  3.44 us
  transfers between devices with their start and end apart: 2, of which 2 were waited for; matrix products, arithmetic and copies ran while one was open for 19% of the time, Pallas kernels for 0%

profile of v1, /device:TPU:0, one launch (start us, length us, event | category | flops | bytes accessed | tf_op | source)
XLA Modules:
  0.0 150.9 jit_solution(11384973944147587020)
XLA Ops:
  6.5 0.0 all-gather.3.cloned.1.call-start
  6.5 0.7 all-gather.3.cloned.1.call-update
  7.3 0.0 all-gather.5.cloned.1.call-start
  7.3 0.7 all-gather.5.cloned.1.call-update
  8.0 1.2 dynamic_slice.3
  9.3 1.3 multiply_exponential_fusion
  10.6 64.2 %all-gather.3.cloned.1.call-done = bf16[1024,2048]{1,0:T(8,128)(2,1)} async-done(((bf16[32,2048]{1,0:T(8,128)(2,1)}), bf16[1024,2048]{1,0:T(8,128)(2,1)}) %all-gather.3.cloned.1.call-update) | async-done | bytes 4194320 | tf_op jit(solution)/shard_map/all_gather | solution.py:24
  74.8 0.0 copy-start
  74.8 3.4 %multiply_convert_fusion = bf16[1024,2048]{1,0:T(8,128)(2,1)S(1)} fusion(bf16[1024,2048]{1,0:T(8,128)(2,1)} %all-gather.3.cloned.1.call-done, f32[2048]{0:T(1024)S(1)} %multiply_exponential_fusion), kind=kLoop, calls=%fused_computation.1 | loop fusion | flops 6291456 | bytes 8396800 | tf_op jit(solution)/shard_map/convert_element_type | solution.py:25
  78.2 0.0 copy-done
  78.2 3.5 %fusion = f32[1024,1024]{1,0:T(8,128)S(1)} fusion(bf16[1024,2048]{1,0:T(8,128)(2,1)S(1)} %multiply_convert_fusion, bf16[1024,2048]{1,0:T(8,128)(2,1)S(1)} %copy-done), kind=kOutput, calls=%fused_computation.4 | convolution fusion | flops 3221225472 | bytes 10485760 | tf_op jit(solution)/shard_map/dot_general | solution.py:13
  81.7 1.3 fusion.3
  83.0 0.1 slice_bitcast_fusion.3
  83.2 0.3 pad_maximum_fusion
  83.4 30.4 %all_to_all.5 = bf16[4,1,256,1024]{2,3,1,0:T(8,128)(2,1)S(1)} all-to-all(bf16[4,1,256,1024]{2,3,1,0:T(8,128)(2,1)S(1)} %pad_maximum_fusion), channel_id=1, replica_groups=mesh['tm'=4,'pts'=8] {'tm'}, dimensions={0} | all-to-all | bytes 4194304 | tf_op jit(solution)/shard_map/all_to_all | solution.py:31
  113.8 0.0 copy-start.1
  113.8 0.0 copy-start.2
  113.8 0.0 copy-start.3
  113.8 2.4 %copy.8 = bf16[4,1,256,1024]{3,2,0,1:T(8,128)(2,1)} copy(bf16[4,1,256,1024]{2,3,1,0:T(8,128)(2,1)S(1)} %all_to_all.5) | data formatting | bytes 4194304 | tf_op jit(solution)/shard_map/all_to_all | solution.py:31
  116.2 3.2 %copy.9 = bf16[1,4,256,1024]{3,1,2,0:T(4,128)(2,1)S(1)} copy(bf16[1,4,256,1024]{3,2,1,0:T(8,128)(2,1)} %bitcast.22) | data formatting | bytes 4194304
  119.4 0.0 copy-done.1
  119.4 0.0 copy-done.2
  119.4 0.0 copy-done.3
  119.4 5.1 %convolution_convert_fusion = bf16[8,262144]{1,0:T(8,128)(2,1)} fusion(bf16[4,262144]{1,0:T(4,128)(2,1)S(1)} %bitcast.21, f32[4]{0:T(128)S(1)} %copy-done.1, f32[8]{0:T(128)S(1)} %copy-done.2, f32[4]{0:T(128)S(1)} %copy-done.3), kind=kOutput, calls=%fused_computation | convolution fusion | flops 102760512 | bytes 6291520 | tf_op jit(solution)/shard_map/dot_general | solution.py:43
  124.5 6.0 %reshape.16 = bf16[2048,1024]{1,0:T(8,128)(2,1)} reshape(bf16[8,262144]{1,0:T(8,128)(2,1)} %convolution_convert_fusion) | data formatting | bytes 8388608 | tf_op jit(solution)/shard_map/reshape | solution.py:44
  130.6 4.1 %all-gather.5.cloned.1.call-done = bf16[1024,1024]{1,0:T(8,128)(2,1)} async-done(((bf16[32,1024]{1,0:T(8,128)(2,1)}), bf16[1024,1024]{1,0:T(8,128)(2,1)}) %all-gather.5.cloned.1.call-update) | async-done | bytes 2097168 | tf_op jit(solution)/shard_map/all_gather | solution.py:45
  134.7 9.4 %convolution_convert_fusion.1 = bf16[2048,1024]{1,0:T(8,128)(2,1)} fusion(bf16[2048,1024]{1,0:T(8,128)(2,1)} %reshape.16, bf16[1024,1024]{1,0:T(8,128)(2,1)} %all-gather.5.cloned.1.call-done), kind=kOutput, calls=%fused_computation.3 | convolution fusion | flops 4297064448 | bytes 10485760 | tf_op jit(solution)/shard_map/dot_general | solution.py:46
Async XLA Ops:
  6.5 68.2 %all-gather.3.cloned.1.call-start = ((), (), s32[]{:S(2)}) async-start(), calls=%async_computation.1 | async-start | bytes 4325376 | tf_op jit(solution)/shard_map/all_gather | solution.py:24
  7.3 127.4 %all-gather.5.cloned.1.call-start = ((), (), s32[]{:S(2)}) async-start(), calls=%async_computation.2 | async-start | bytes 2162688 | tf_op jit(solution)/shard_map/all_gather | solution.py:45
  74.8 3.5 %copy-start = (bf16[1024,2048]{1,0:T(8,128)(2,1)S(1)}, bf16[1024,2048]{1,0:T(8,128)(2,1)}, u32[]{:S(2)}) copy-start(bf16[1024,2048]{1,0:T(8,128)(2,1)} %param.7) | copy-start | bytes 12582916
  113.8 5.6 %copy-start.1 = (f32[4]{0:T(128)S(1)}, f32[4]{0:T(128)}, u32[]{:S(2)}) copy-start(f32[4]{0:T(128)} %param.10) | copy-start | bytes 52
  113.8 5.6 %copy-start.2 = (f32[8]{0:T(128)S(1)}, f32[8]{0:T(128)}, u32[]{:S(2)}) copy-start(f32[8]{0:T(128)} %param.12) | copy-start | bytes 100
  113.8 5.6 %copy-start.3 = (f32[4]{0:T(128)S(1)}, f32[4]{0:T(128)}, u32[]{:S(2)}) copy-start(f32[4]{0:T(128)} %param.11) | copy-start | bytes 52
Sparse Core Ops, SparseCore 0:
  10.3 64.3 all-gather.2
  77.7 56.8 all-gather.4
